TPU v7x, 256 devices: a whole 4x4x8 slice. The times are simulated.
256 devices in a mesh: batch: 2 (over x_hi), head: 8 (over y, x_lo), blk: 16 (over z, core).
Axes of the slice: x: 4 (x_hi: 2, x_lo: 2; x = x_hi * 2 + x_lo), y: 4, z: 8, core: 2. Of those that a mesh axis runs over, the one named last changes fastest.
Arguments:
- tokens: bfloat16 [32, 2048, 1024], P(('batch', 'blk'), 'head'), parts along dimension 0, may hold values from -10.5 to 10.5
- proj_weight: bfloat16 [1024, 3072], replicated, may hold values from -0.1875 to 0.1875
- out_weight: bfloat16 [1024, 1024], replicated, may hold values from -1.5 to 1.5
- pattern: int32 [512, 16], P(('batch', 'blk')), parts along dimension 0, may hold values from 0 to 255, as said below
Outputs:
- mixed_out: bfloat16 [32, 2048, 1024], P(('batch', 'blk'), 'head'), parts along dimension 0
There are 2 independent parts, one for each index of `batch`. A program takes and returns all parts, laid end to end along the dimension named above; an argument that names none is the same for every part. Nothing has to cross between parts.
Inputs may be any that keep to these rules, and one draw needn't show every extreme that they name: `pattern`: row i lists first 6 distinct blocks j with |j - i| <= 8, among them i itself, then 10 distinct summary blocks j (j % 16 >= 12) with |j - i| > 8. Every row with 8 <= i < 248 lists i - 8 and i + 8.
All inputs are finite; a program needn't handle non-finite values.
Results may differ from a plain program's by a relative error of at most 0.0095.
Values may be sent and summed in bfloat16 or wider, within the bound.
A program may use at most 128 MiB of HBM per device.

v0:
```python
import jax
import jax.numpy as jnp
from jax import lax
from jax.sharding import PartitionSpec as P

D = 1024
H = 16
HD = 64
BLK = 128
TOK_DEV = 2048
SB = 16
KSEL = 16


def on_device(tokens, proj_weight, out_weight, pattern):
    heads_axis = lax.axis_size("head")
    local_heads = H // heads_axis
    head_width = local_heads * HD
    col_width = local_heads * 3 * HD
    own_rows = tokens[0]
    local_tokens = own_rows.shape[0]
    start_col = lax.axis_index("head") * col_width
    columns = lax.dynamic_slice_in_dim(proj_weight, start_col, col_width, 1)
    columns = columns.reshape(D, local_heads, 3, HD).transpose(0, 2, 1, 3).reshape(D, col_width)
    projected = jnp.dot(
        lax.all_gather(own_rows, "head", axis=0, tiled=True),
        columns,
        preferred_element_type=jnp.float32,
    ).astype(jnp.bfloat16)
    queries = projected[:, :head_width]
    key_value = projected[:, head_width:]
    source = lax.all_gather(key_value, "blk", axis=0, tiled=True)
    source_blocks = source.reshape(-1, BLK, 2 * head_width)
    group_size = 4
    group_count = SB // group_size
    query_groups = queries.reshape(group_count, group_size, BLK, head_width)
    position_groups = pattern.reshape(group_count, group_size, KSEL)
    score_scale = HD ** (-0.5)
    lane_head = lax.broadcasted_iota(jnp.int32, (1, 1, head_width), 2) // HD

    def attend(operands):
        query_group, positions = operands
        picked = source_blocks[positions].reshape(group_size, KSEL * BLK, 2 * head_width)
        key_rows = picked[:, :, :head_width]
        value_rows = picked[:, :, head_width:]
        total = jnp.zeros((group_size, BLK, head_width), jnp.float32)
        for which in range(local_heads):
            inside = lane_head == which
            masked = jnp.where(inside, query_group, jnp.zeros_like(query_group))
            scores = (
                jnp.einsum("gqc,gkc->gqk", masked, key_rows, preferred_element_type=jnp.float32)
                * score_scale
            )
            row_max = jnp.max(scores, axis=-1, keepdims=True)
            raised = jnp.exp(scores - row_max)
            weights = (raised / jnp.sum(raised, axis=-1, keepdims=True)).astype(jnp.bfloat16)
            product = jnp.einsum(
                "gqk,gkc->gqc", weights, value_rows, preferred_element_type=jnp.float32
            )
            total = total + jnp.where(inside, product, 0.0)
        return total.astype(jnp.bfloat16)

    attended = lax.map(attend, (query_groups, position_groups))
    attended = attended.reshape(TOK_DEV, head_width)
    token_heads = lax.all_to_all(attended, "head", split_axis=0, concat_axis=1, tiled=True)
    mixed_out = jnp.dot(token_heads, out_weight, preferred_element_type=jnp.float32).astype(
        jnp.bfloat16
    )
    return mixed_out.reshape(1, local_tokens, D)


def solution(mesh):
    return jax.shard_map(
        on_device,
        mesh=mesh,
        in_specs=(P(("batch", "blk"), "head", None), P(), P(), P(("batch", "blk"), None)),
        out_specs=P(("batch", "blk"), "head", None),
        check_vma=False,
    )
```

profile of v0, /device:TPU:1, one launch (start us, length us, event | category | flops | bytes accessed | tf_op | source)
XLA Modules:
  0.0 347.2 jit_solution(8824220184311968826)
XLA Ops:
  6.5 0.0 copy-start
  6.5 0.0 all-gather.6.cloned.1.call-start
  6.5 0.7 all-gather.6.cloned.1.call-update
  7.3 0.0 all-gather.4.cloned.1.call-start
  7.3 1.2 constant_dynamic-slice_fusion
  8.5 1.2 copy.18
  9.7 1.2 copy.12
  10.9 95.1 %all-gather.6.cloned.1.call-done = bf16[1,2048,1024]{2,1,0:T(8,128)(2,1)} async-done(((bf16[1,256,1024]{2,1,0:T(8,128)(2,1)}), bf16[1,2048,1024]{2,1,0:T(8,128)(2,1)}) %all-gather.6.cloned.1.call-update) | async-done | bytes 4194320 | tf_op jit(solution)/shard_map/all_gather | solution.py:26
  106.0 4.0 %fusion.111 = bf16[2048,384]{0,1:T(8,128)(2,1)S(1)} fusion(bf16[1024,384]{0,1:T(8,128)(2,1)S(1)} %bitcast.86, bf16[1,2048,1024]{2,1,0:T(8,128)(2,1)} %all-gather.6.cloned.1.call-done), kind=kOutput, calls=%fused_computation.67 | convolution fusion | flops 1611399168 | bytes 6553600 | tf_op jit(solution)/shard_map/dot_general | solution.py:25
  110.0 1.1 copy-done.1
  111.2 1.1 slice.23
  112.3 0.0 all-gather.4.cloned.1.call-update
  112.3 1.1 slice.22
  113.4 0.3 copy.16
  113.6 94.8 %all-gather.4.cloned.1.call-done = bf16[32768,256]{0,1:T(8,128)(2,1)} async-done(((bf16[2048,256]{0,1:T(8,128)(2,1)}), bf16[32768,256]{0,1:T(8,128)(2,1)}) %all-gather.4.cloned.1.call-update) | async-done | bytes 16777232 | tf_op jit(solution)/shard_map/all_gather | solution.py:32
  208.5 22.4 %copy.17 = bf16[32768,256]{1,0:T(8,128)(2,1)} copy(bf16[32768,256]{0,1:T(8,128)(2,1)} %all-gather.4.cloned.1.call-done) | data formatting | bytes 33554432
  230.9 93.5 %while.12 = (s32[]{:T(128)}, bf16[4,4,128,128]{3,2,1,0:T(8,128)(2,1)}, bf16[4,4,128,128]{3,2,1,0:T(8,128)(2,1)S(1)}, s32[4,4,16]{2,1,0:T(4,128)}, bf16[256,128,256]{2,1,0:T(8,128)(2,1)}, /*index=5*/s32[]{:T(128)}) while((s32[]{:T(128)}, bf16[4,4,128,128]{3,2,1,0:T(8,128)(2,1)}, bf16[4,4,128,128]{3,2,1,0:T(8,128)(2,1)S(1)}, ...), condition=%wide.region_5.6_spmd.clone.clone, body=%wide.region_0.5_spmd.clone.clone.sunk | while | flops 1625828864 | bytes 22169436 | solution.py:63
  230.9 0.7 compare_select_fusion.2
  231.6 0.1 reshape.157
  231.7 8.5 %gather_fusion = bf16[64,128,256]{2,1,0:T(8,128)(2,1)} fusion(bf16[256,128,256]{2,1,0:T(8,128)(2,1)} %get-tuple-element.155, s32[1024]{0:T(1024)S(1)} %pad_clamp_fusion.2), kind=kCustom, calls=%fused_computation.clone.clone.1 | custom fusion | bytes 8388864 | tf_op jit(solution)/shard_map/while/body/eval_jaxpr/gather | solution.py:43
  240.2 2.9 fusion.146
  243.1 2.9 fusion.144
  246.0 3.8 %fusion.145 = f32[4,128,128]{2,1,0:T(8,128)S(1)} fusion(bf16[4,2048,256]{2,1,0:T(8,128)(2,1)} %bitcast.80, f32[4,128]{1,0:T(4,128)S(1)} %fusion.144, pred[128]{0:T(512)(128)(4,1)S(1)} %get-tuple-element.137, bf16[4,4,128,128]{3,2,1,0:T(8,128)(2,1)S(1)} %get-tuple-element.153, s32[]{:T(128)S(6)} %copy.22), kind=kOutput, calls=%fused_computation.25.clone.1 | convolution fusion | flops 541198848 | bytes 4590596 | tf_op jit(solution)/shard_map/while/body/eval_jaxpr/gqk,gkc->gqc/dot_general | solution.py:57
  249.8 4.5 %fusion.147 = bf16[4,4,128,128]{3,2,1,0:T(8,128)(2,1)} fusion(bf16[4,4,128,128]{3,2,1,0:T(8,128)(2,1)} %get-tuple-element.146, s32[]{:T(128)S(6)} %copy.22, f32[4,128,128]{2,1,0:T(8,128)S(1)} %fusion.145, bf16[4,2048,256]{2,1,0:T(8,128)(2,1)} %bitcast.81, f32[4,128]{1,0:T(4,128)S(1)} %fusion.146, pred[128]{0:T(512)(128)(4,1)S(1)} %get-tuple-element.138, ...), kind=kOutput, calls=%fused_computation.27.clone.1 | convolution fusion | flops 541329920 | bytes 4722688 | tf_op jit(solution)/shard_map/while/body/eval_jaxpr/gqk,gkc->gqc/dot_general | solution.py:57
  254.3 0.7 compare_select_fusion.2
  254.9 0.1 reshape.157
  255.0 8.5 %gather_fusion = bf16[64,128,256]{2,1,0:T(8,128)(2,1)} fusion(bf16[256,128,256]{2,1,0:T(8,128)(2,1)} %get-tuple-element.155, s32[1024]{0:T(1024)S(1)} %pad_clamp_fusion.2), kind=kCustom, calls=%fused_computation.clone.clone.1 | custom fusion | bytes 8388864 | tf_op jit(solution)/shard_map/while/body/eval_jaxpr/gather | solution.py:43
  263.5 2.9 fusion.146
  266.4 2.9 fusion.144
  269.3 3.8 %fusion.145 = f32[4,128,128]{2,1,0:T(8,128)S(1)} fusion(bf16[4,2048,256]{2,1,0:T(8,128)(2,1)} %bitcast.80, f32[4,128]{1,0:T(4,128)S(1)} %fusion.144, pred[128]{0:T(512)(128)(4,1)S(1)} %get-tuple-element.137, bf16[4,4,128,128]{3,2,1,0:T(8,128)(2,1)S(1)} %get-tuple-element.153, s32[]{:T(128)S(6)} %copy.22), kind=kOutput, calls=%fused_computation.25.clone.1 | convolution fusion | flops 541198848 | bytes 4590596 | tf_op jit(solution)/shard_map/while/body/eval_jaxpr/gqk,gkc->gqc/dot_general | solution.py:57
  273.1 4.5 %fusion.147 = bf16[4,4,128,128]{3,2,1,0:T(8,128)(2,1)} fusion(bf16[4,4,128,128]{3,2,1,0:T(8,128)(2,1)} %get-tuple-element.146, s32[]{:T(128)S(6)} %copy.22, f32[4,128,128]{2,1,0:T(8,128)S(1)} %fusion.145, bf16[4,2048,256]{2,1,0:T(8,128)(2,1)} %bitcast.81, f32[4,128]{1,0:T(4,128)S(1)} %fusion.146, pred[128]{0:T(512)(128)(4,1)S(1)} %get-tuple-element.138, ...), kind=kOutput, calls=%fused_computation.27.clone.1 | convolution fusion | flops 541329920 | bytes 4722688 | tf_op jit(solution)/shard_map/while/body/eval_jaxpr/gqk,gkc->gqc/dot_general | solution.py:57
  277.6 0.7 compare_select_fusion.2
  278.3 0.1 reshape.157
  278.4 8.5 %gather_fusion = bf16[64,128,256]{2,1,0:T(8,128)(2,1)} fusion(bf16[256,128,256]{2,1,0:T(8,128)(2,1)} %get-tuple-element.155, s32[1024]{0:T(1024)S(1)} %pad_clamp_fusion.2), kind=kCustom, calls=%fused_computation.clone.clone.1 | custom fusion | bytes 8388864 | tf_op jit(solution)/shard_map/while/body/eval_jaxpr/gather | solution.py:43
  286.9 2.9 fusion.146
  289.8 2.9 fusion.144
  292.7 3.8 %fusion.145 = f32[4,128,128]{2,1,0:T(8,128)S(1)} fusion(bf16[4,2048,256]{2,1,0:T(8,128)(2,1)} %bitcast.80, f32[4,128]{1,0:T(4,128)S(1)} %fusion.144, pred[128]{0:T(512)(128)(4,1)S(1)} %get-tuple-element.137, bf16[4,4,128,128]{3,2,1,0:T(8,128)(2,1)S(1)} %get-tuple-element.153, s32[]{:T(128)S(6)} %copy.22), kind=kOutput, calls=%fused_computation.25.clone.1 | convolution fusion | flops 541198848 | bytes 4590596 | tf_op jit(solution)/shard_map/while/body/eval_jaxpr/gqk,gkc->gqc/dot_general | solution.py:57
  296.5 4.5 %fusion.147 = bf16[4,4,128,128]{3,2,1,0:T(8,128)(2,1)} fusion(bf16[4,4,128,128]{3,2,1,0:T(8,128)(2,1)} %get-tuple-element.146, s32[]{:T(128)S(6)} %copy.22, f32[4,128,128]{2,1,0:T(8,128)S(1)} %fusion.145, bf16[4,2048,256]{2,1,0:T(8,128)(2,1)} %bitcast.81, f32[4,128]{1,0:T(4,128)S(1)} %fusion.146, pred[128]{0:T(512)(128)(4,1)S(1)} %get-tuple-element.138, ...), kind=kOutput, calls=%fused_computation.27.clone.1 | convolution fusion | flops 541329920 | bytes 4722688 | tf_op jit(solution)/shard_map/while/body/eval_jaxpr/gqk,gkc->gqc/dot_general | solution.py:57
  301.0 0.7 compare_select_fusion.2
  301.7 0.1 reshape.157
  301.8 8.5 %gather_fusion = bf16[64,128,256]{2,1,0:T(8,128)(2,1)} fusion(bf16[256,128,256]{2,1,0:T(8,128)(2,1)} %get-tuple-element.155, s32[1024]{0:T(1024)S(1)} %pad_clamp_fusion.2), kind=kCustom, calls=%fused_computation.clone.clone.1 | custom fusion | bytes 8388864 | tf_op jit(solution)/shard_map/while/body/eval_jaxpr/gather | solution.py:43
  310.3 2.9 fusion.146
  313.2 2.9 fusion.144
  316.1 3.8 %fusion.145 = f32[4,128,128]{2,1,0:T(8,128)S(1)} fusion(bf16[4,2048,256]{2,1,0:T(8,128)(2,1)} %bitcast.80, f32[4,128]{1,0:T(4,128)S(1)} %fusion.144, pred[128]{0:T(512)(128)(4,1)S(1)} %get-tuple-element.137, bf16[4,4,128,128]{3,2,1,0:T(8,128)(2,1)S(1)} %get-tuple-element.153, s32[]{:T(128)S(6)} %copy.22), kind=kOutput, calls=%fused_computation.25.clone.1 | convolution fusion | flops 541198848 | bytes 4590596 | tf_op jit(solution)/shard_map/while/body/eval_jaxpr/gqk,gkc->gqc/dot_general | solution.py:57
  319.9 4.5 %fusion.147 = bf16[4,4,128,128]{3,2,1,0:T(8,128)(2,1)} fusion(bf16[4,4,128,128]{3,2,1,0:T(8,128)(2,1)} %get-tuple-element.146, s32[]{:T(128)S(6)} %copy.22, f32[4,128,128]{2,1,0:T(8,128)S(1)} %fusion.145, bf16[4,2048,256]{2,1,0:T(8,128)(2,1)} %bitcast.81, f32[4,128]{1,0:T(4,128)S(1)} %fusion.146, pred[128]{0:T(512)(128)(4,1)S(1)} %get-tuple-element.138, ...), kind=kOutput, calls=%fused_computation.27.clone.1 | convolution fusion | flops 541329920 | bytes 4722688 | tf_op jit(solution)/shard_map/while/body/eval_jaxpr/gqk,gkc->gqc/dot_general | solution.py:57
  324.4 14.3 %all_to_all.19 = bf16[8,256,128]{2,1,0:T(8,128)(2,1)S(1)} all-to-all(bf16[8,256,128]{2,1,0:T(8,128)(2,1)} %bitcast.88), channel_id=1, replica_groups=mesh['batch'=2,'head'=8,'blk'=16] {'head'}, dimensions={0} | all-to-all | bytes 1048576 | tf_op jit(solution)/shard_map/all_to_all | solution.py:65
  338.6 0.2 copy.15
  338.8 1.5 fusion.114
  (11 shorter events, 0.1 us)
Async XLA Ops:
  6.5 332.3 %copy-start = (bf16[1024,1024]{1,0:T(8,128)(2,1)S(1)}, bf16[1024,1024]{1,0:T(8,128)(2,1)}, u32[]{:S(2)}) copy-start(bf16[1024,1024]{1,0:T(8,128)(2,1)} %param.8) | copy-start | bytes 6291460
  6.5 99.5 %all-gather.6.cloned.1.call-start = ((), (), s32[]{:S(2)}) async-start(), calls=%async_computation.2 | async-start | bytes 4718592 | tf_op jit(solution)/shard_map/all_gather | solution.py:26
  7.3 201.2 %all-gather.4.cloned.1.call-start = ((), (), s32[]{:S(2)}) async-start(), calls=%async_computation.1 | async-start | bytes 17825792 | tf_op jit(solution)/shard_map/all_gather | solution.py:32
  110.0 1.2 copy-start.1
Sparse Core Ops, SparseCore 0:
  9.1 96.8 all-gather.5
  112.4 96.0 all-gather.3
where the time goes:
time: 349 us; the launch traced here: 347 us
  waiting for transfers between devices  191 us (55%)
  local copies, waits for them, and re-layouts  64.1 us (18%)
  matrix products  61.8 us (18%)
  blocking collectives  14.3 us (4%)
  between operations  13.5 us (4%)
    all_gather x1, waiting for transfers between devices, on_device(): lax.all_gather(own_rows, 'head', axis=0, tiled=True)  95.1 us
    all_gather x1, waiting for transfers between devices, on_device(): source = lax.all_gather(key_value, 'blk', axis=0, tiled=True)  94.8 us
    gather x4, local copies, waits for them, and re-layouts, attend(): source_blocks[positions].reshape(group_size, KSEL * BLK, 2 * head_width)  34 us
    dot_general x8, matrix products, attend(): jnp.einsum('gqk,gkc->gqc', weights, value_rows, preferred_element_type=jn...  33.1 us
    unnamed x7, local copies, waits for them, and re-layouts  25 us
    sub x8, matrix products, attend(): raised = jnp.exp(scores - row_max)  23.2 us
    all_to_all x1, blocking collectives, on_device(): lax.all_to_all(attended, 'head', split_axis=0, concat_axis=1, tiled=True)  14.3 us
  transfers between devices with their start and end apart: 2, of which 2 were waited for; matrix products, arithmetic and copies ran while one was open for 1% of the time, Pallas kernels for 0%

commit v1 on v0

--- a/solution.py
+++ b/solution.py
@@ -23,7 +23,9 @@
     columns = lax.dynamic_slice_in_dim(proj_weight, start_col, col_width, 1)
     columns = columns.reshape(D, local_heads, 3, HD).transpose(0, 2, 1, 3).reshape(D, col_width)
     projected = jnp.dot(
-        lax.all_gather(own_rows, "head", axis=0, tiled=True),
+        jnp.concatenate(
+            lax.all_to_all(jnp.stack([own_rows] * lax.axis_size("head")), "head", 0, 0), axis=0
+        ),
         columns,
         preferred_element_type=jnp.float32,
     ).astype(jnp.bfloat16)

time: 349 us -> 309 us (0.89)
  waiting for transfers between devices: 191 us -> 142 us
  starting transfers between devices: 0.04 us -> 5.98 us
  local copies, waits for them, and re-layouts: 64.1 us -> 67.9 us
    all_gather x1 -> x0, waiting for transfers between devices: 95.1 us -> none  [on_device(): lax.all_gather(own_rows, 'head', axis=0, tiled=True)]
    all_to_all x0 -> x1, waiting for transfers between devices: none -> 44.1 us  [on_device(): lax.all_to_all(jnp.stack([own_rows] * lax.axis_size('head')), 'head', 0, 0)]
    all_to_all x0 -> x1, starting transfers between devices: none -> 5.95 us  [on_device(): lax.all_to_all(jnp.stack([own_rows] * lax.axis_size('head')), 'head', 0, 0)]
    another operation x0 -> x1, local copies, waits for them, and re-layouts: none -> 3.7 us  [on_device(): jnp.stack([own_rows] * lax.axis_size('head'))]
  transfers between devices with their start and end apart: 2 -> 2, of which waited for: 2 -> 2; matrix products, arithmetic and copies ran while one was open for 1% -> 2% of each run, Pallas kernels for 0% -> 0%
where the time goes in v1:
time: 309 us; the launch traced here: 308 us
  waiting for transfers between devices  142 us (46%)
  local copies, waits for them, and re-layouts  67.9 us (22%)
  matrix products  61.8 us (20%)
  blocking collectives  14.3 us (5%)
  between operations  13.5 us (4%)
  starting transfers between devices  5.98 us (2%)
    all_gather x1, waiting for transfers between devices, on_device(): source = lax.all_gather(key_value, 'blk', axis=0, tiled=True)  97.5 us
    all_to_all x1, waiting for transfers between devices, on_device(): lax.all_to_all(jnp.stack([own_rows] * lax.axis_size('head')), 'head', 0, 0)  44.1 us
    gather x4, local copies, waits for them, and re-layouts, attend(): source_blocks[positions].reshape(group_size, KSEL * BLK, 2 * head_width)  34 us
    dot_general x8, matrix products, attend(): jnp.einsum('gqk,gkc->gqc', weights, value_rows, preferred_element_type=jn...  33.1 us
    unnamed x7, local copies, waits for them, and re-layouts  25.1 us
    sub x8, matrix products, attend(): raised = jnp.exp(scores - row_max)  23.2 us
    all_to_all x1, blocking collectives, on_device(): lax.all_to_all(attended, 'head', split_axis=0, concat_axis=1, tiled=True)  14.3 us
  transfers between devices with their start and end apart: 2, of which 2 were waited for; matrix products, arithmetic and copies ran while one was open for 2% of the time, Pallas kernels for 0%

profile of v1, /device:TPU:1, one launch (start us, length us, event | category | flops | bytes accessed | tf_op | source)
XLA Modules:
  0.0 307.9 jit_solution(15817231137070274681)
XLA Ops:
  6.5 3.7 %stack.3 = bf16[8,256,1024]{2,1,0:T(8,128)(2,1)} broadcast(bf16[256,1024]{1,0:T(8,128)(2,1)} %bitcast.83), dimensions={1,2} | broadcast | bytes 4718592 | tf_op jit(solution)/shard_map/stack | solution.py:27
  10.2 5.9 %all-to-all-start = ((bf16[8,256,1024]{2,1,0:T(8,128)(2,1)}), bf16[8,256,1024]{2,1,0:T(8,128)(2,1)}, u32[]{:S(2)}, u32[]{:S(2)}) async-start(bf16[8,256,1024]{2,1,0:T(8,128)(2,1)} %stack.3), calls=%async_computation | async-start | bytes 8388608 | tf_op jit(solution)/shard_map/all_to_all | solution.py:27
  16.2 0.0 all-gather.2.cloned.1.call-start
  16.2 1.2 constant_dynamic-slice_fusion
  17.5 1.2 copy.18
  18.7 1.2 copy.12
  19.9 44.1 %all-to-all-done = bf16[8,256,1024]{2,1,0:T(8,128)(2,1)} async-done(((bf16[8,256,1024]{2,1,0:T(8,128)(2,1)}), bf16[8,256,1024]{2,1,0:T(8,128)(2,1)}, u32[]{:S(2)}, u32[]{:S(2)}) %all-to-all-start) | async-done | bytes 4194336 | tf_op jit(solution)/shard_map/all_to_all | solution.py:27
  64.0 4.0 %fusion.106 = bf16[2048,384]{0,1:T(8,128)(2,1)S(1)} fusion(bf16[1024,384]{0,1:T(8,128)(2,1)S(1)} %bitcast.82, bf16[2048,1024]{1,0:T(8,128)(2,1)} %bitcast.4), kind=kOutput, calls=%fused_computation.65 | convolution fusion | flops 1611399168 | bytes 6553600 | tf_op jit(solution)/shard_map/dot_general | solution.py:25
  68.0 1.1 copy-done.1
  69.2 1.1 slice.23
  70.3 0.0 all-gather.2.cloned.1.call-update
  70.3 1.1 slice.22
  71.4 0.3 copy.16
  71.6 97.5 %all-gather.2.cloned.1.call-done = bf16[32768,256]{0,1:T(8,128)(2,1)} async-done(((bf16[2048,256]{0,1:T(8,128)(2,1)}), bf16[32768,256]{0,1:T(8,128)(2,1)}) %all-gather.2.cloned.1.call-update) | async-done | bytes 16777232 | tf_op jit(solution)/shard_map/all_gather | solution.py:34
  169.2 22.4 %copy.17 = bf16[32768,256]{1,0:T(8,128)(2,1)} copy(bf16[32768,256]{0,1:T(8,128)(2,1)} %all-gather.2.cloned.1.call-done) | data formatting | bytes 33554432
  191.6 93.5 %while.12 = (s32[]{:T(128)}, bf16[4,4,128,128]{3,2,1,0:T(8,128)(2,1)}, bf16[4,4,128,128]{3,2,1,0:T(8,128)(2,1)S(1)}, s32[4,4,16]{2,1,0:T(4,128)}, bf16[256,128,256]{2,1,0:T(8,128)(2,1)}, /*index=5*/s32[]{:T(128)}) while((s32[]{:T(128)}, bf16[4,4,128,128]{3,2,1,0:T(8,128)(2,1)}, bf16[4,4,128,128]{3,2,1,0:T(8,128)(2,1)S(1)}, ...), condition=%wide.region_5.6_spmd.clone.clone, body=%wide.region_0.5_spmd.clone.clone.sunk | while | flops 1625828864 | bytes 22169436 | solution.py:65
  191.6 0.7 compare_select_fusion.2
  192.3 0.1 reshape.161
  192.4 8.5 %gather_fusion = bf16[64,128,256]{2,1,0:T(8,128)(2,1)} fusion(bf16[256,128,256]{2,1,0:T(8,128)(2,1)} %get-tuple-element.155, s32[1024]{0:T(1024)S(1)} %pad_clamp_fusion.2), kind=kCustom, calls=%fused_computation.clone.clone.1 | custom fusion | bytes 8388864 | tf_op jit(solution)/shard_map/while/body/eval_jaxpr/gather | solution.py:45
  200.9 2.9 fusion.140
  203.8 2.9 fusion.138
  206.7 3.8 %fusion.139 = f32[4,128,128]{2,1,0:T(8,128)S(1)} fusion(bf16[4,2048,256]{2,1,0:T(8,128)(2,1)} %bitcast.76, f32[4,128]{1,0:T(4,128)S(1)} %fusion.138, pred[128]{0:T(512)(128)(4,1)S(1)} %get-tuple-element.137, bf16[4,4,128,128]{3,2,1,0:T(8,128)(2,1)S(1)} %get-tuple-element.153, s32[]{:T(128)S(6)} %copy.22), kind=kOutput, calls=%fused_computation.25.clone.1 | convolution fusion | flops 541198848 | bytes 4590596 | tf_op jit(solution)/shard_map/while/body/eval_jaxpr/gqk,gkc->gqc/dot_general | solution.py:59
  210.5 4.5 %fusion.141 = bf16[4,4,128,128]{3,2,1,0:T(8,128)(2,1)} fusion(bf16[4,4,128,128]{3,2,1,0:T(8,128)(2,1)} %get-tuple-element.146, s32[]{:T(128)S(6)} %copy.22, f32[4,128,128]{2,1,0:T(8,128)S(1)} %fusion.139, bf16[4,2048,256]{2,1,0:T(8,128)(2,1)} %bitcast.77, f32[4,128]{1,0:T(4,128)S(1)} %fusion.140, pred[128]{0:T(512)(128)(4,1)S(1)} %get-tuple-element.138, ...), kind=kOutput, calls=%fused_computation.27.clone.1 | convolution fusion | flops 541329920 | bytes 4722688 | tf_op jit(solution)/shard_map/while/body/eval_jaxpr/gqk,gkc->gqc/dot_general | solution.py:59
  215.0 0.7 compare_select_fusion.2
  215.7 0.1 reshape.161
  215.7 8.5 %gather_fusion = bf16[64,128,256]{2,1,0:T(8,128)(2,1)} fusion(bf16[256,128,256]{2,1,0:T(8,128)(2,1)} %get-tuple-element.155, s32[1024]{0:T(1024)S(1)} %pad_clamp_fusion.2), kind=kCustom, calls=%fused_computation.clone.clone.1 | custom fusion | bytes 8388864 | tf_op jit(solution)/shard_map/while/body/eval_jaxpr/gather | solution.py:45
  224.3 2.9 fusion.140
  227.2 2.9 fusion.138
  230.1 3.8 %fusion.139 = f32[4,128,128]{2,1,0:T(8,128)S(1)} fusion(bf16[4,2048,256]{2,1,0:T(8,128)(2,1)} %bitcast.76, f32[4,128]{1,0:T(4,128)S(1)} %fusion.138, pred[128]{0:T(512)(128)(4,1)S(1)} %get-tuple-element.137, bf16[4,4,128,128]{3,2,1,0:T(8,128)(2,1)S(1)} %get-tuple-element.153, s32[]{:T(128)S(6)} %copy.22), kind=kOutput, calls=%fused_computation.25.clone.1 | convolution fusion | flops 541198848 | bytes 4590596 | tf_op jit(solution)/shard_map/while/body/eval_jaxpr/gqk,gkc->gqc/dot_general | solution.py:59
  233.9 4.5 %fusion.141 = bf16[4,4,128,128]{3,2,1,0:T(8,128)(2,1)} fusion(bf16[4,4,128,128]{3,2,1,0:T(8,128)(2,1)} %get-tuple-element.146, s32[]{:T(128)S(6)} %copy.22, f32[4,128,128]{2,1,0:T(8,128)S(1)} %fusion.139, bf16[4,2048,256]{2,1,0:T(8,128)(2,1)} %bitcast.77, f32[4,128]{1,0:T(4,128)S(1)} %fusion.140, pred[128]{0:T(512)(128)(4,1)S(1)} %get-tuple-element.138, ...), kind=kOutput, calls=%fused_computation.27.clone.1 | convolution fusion | flops 541329920 | bytes 4722688 | tf_op jit(solution)/shard_map/while/body/eval_jaxpr/gqk,gkc->gqc/dot_general | solution.py:59
  238.3 0.7 compare_select_fusion.2
  239.0 0.1 reshape.161
  239.1 8.5 %gather_fusion = bf16[64,128,256]{2,1,0:T(8,128)(2,1)} fusion(bf16[256,128,256]{2,1,0:T(8,128)(2,1)} %get-tuple-element.155, s32[1024]{0:T(1024)S(1)} %pad_clamp_fusion.2), kind=kCustom, calls=%fused_computation.clone.clone.1 | custom fusion | bytes 8388864 | tf_op jit(solution)/shard_map/while/body/eval_jaxpr/gather | solution.py:45
  247.6 2.9 fusion.140
  250.5 2.9 fusion.138
  253.4 3.8 %fusion.139 = f32[4,128,128]{2,1,0:T(8,128)S(1)} fusion(bf16[4,2048,256]{2,1,0:T(8,128)(2,1)} %bitcast.76, f32[4,128]{1,0:T(4,128)S(1)} %fusion.138, pred[128]{0:T(512)(128)(4,1)S(1)} %get-tuple-element.137, bf16[4,4,128,128]{3,2,1,0:T(8,128)(2,1)S(1)} %get-tuple-element.153, s32[]{:T(128)S(6)} %copy.22), kind=kOutput, calls=%fused_computation.25.clone.1 | convolution fusion | flops 541198848 | bytes 4590596 | tf_op jit(solution)/shard_map/while/body/eval_jaxpr/gqk,gkc->gqc/dot_general | solution.py:59
  257.2 4.5 %fusion.141 = bf16[4,4,128,128]{3,2,1,0:T(8,128)(2,1)} fusion(bf16[4,4,128,128]{3,2,1,0:T(8,128)(2,1)} %get-tuple-element.146, s32[]{:T(128)S(6)} %copy.22, f32[4,128,128]{2,1,0:T(8,128)S(1)} %fusion.139, bf16[4,2048,256]{2,1,0:T(8,128)(2,1)} %bitcast.77, f32[4,128]{1,0:T(4,128)S(1)} %fusion.140, pred[128]{0:T(512)(128)(4,1)S(1)} %get-tuple-element.138, ...), kind=kOutput, calls=%fused_computation.27.clone.1 | convolution fusion | flops 541329920 | bytes 4722688 | tf_op jit(solution)/shard_map/while/body/eval_jaxpr/gqk,gkc->gqc/dot_general | solution.py:59
  261.7 0.7 compare_select_fusion.2
  262.4 0.1 reshape.161
  262.5 8.5 %gather_fusion = bf16[64,128,256]{2,1,0:T(8,128)(2,1)} fusion(bf16[256,128,256]{2,1,0:T(8,128)(2,1)} %get-tuple-element.155, s32[1024]{0:T(1024)S(1)} %pad_clamp_fusion.2), kind=kCustom, calls=%fused_computation.clone.clone.1 | custom fusion | bytes 8388864 | tf_op jit(solution)/shard_map/while/body/eval_jaxpr/gather | solution.py:45
  271.0 2.9 fusion.140
  273.9 2.9 fusion.138
  276.8 3.8 %fusion.139 = f32[4,128,128]{2,1,0:T(8,128)S(1)} fusion(bf16[4,2048,256]{2,1,0:T(8,128)(2,1)} %bitcast.76, f32[4,128]{1,0:T(4,128)S(1)} %fusion.138, pred[128]{0:T(512)(128)(4,1)S(1)} %get-tuple-element.137, bf16[4,4,128,128]{3,2,1,0:T(8,128)(2,1)S(1)} %get-tuple-element.153, s32[]{:T(128)S(6)} %copy.22), kind=kOutput, calls=%fused_computation.25.clone.1 | convolution fusion | flops 541198848 | bytes 4590596 | tf_op jit(solution)/shard_map/while/body/eval_jaxpr/gqk,gkc->gqc/dot_general | solution.py:59
  280.6 4.5 %fusion.141 = bf16[4,4,128,128]{3,2,1,0:T(8,128)(2,1)} fusion(bf16[4,4,128,128]{3,2,1,0:T(8,128)(2,1)} %get-tuple-element.146, s32[]{:T(128)S(6)} %copy.22, f32[4,128,128]{2,1,0:T(8,128)S(1)} %fusion.139, bf16[4,2048,256]{2,1,0:T(8,128)(2,1)} %bitcast.77, f32[4,128]{1,0:T(4,128)S(1)} %fusion.140, pred[128]{0:T(512)(128)(4,1)S(1)} %get-tuple-element.138, ...), kind=kOutput, calls=%fused_computation.27.clone.1 | convolution fusion | flops 541329920 | bytes 4722688 | tf_op jit(solution)/shard_map/while/body/eval_jaxpr/gqk,gkc->gqc/dot_general | solution.py:59
  285.1 14.3 %all_to_all.24 = bf16[8,256,128]{2,1,0:T(8,128)(2,1)S(1)} all-to-all(bf16[8,256,128]{2,1,0:T(8,128)(2,1)} %bitcast.85), channel_id=1, replica_groups=mesh['batch'=2,'head'=8,'blk'=16] {'head'}, dimensions={0} | all-to-all | bytes 1048576 | tf_op jit(solution)/shard_map/all_to_all | solution.py:67
  299.3 0.2 copy.15
  299.5 0.0 copy-done
  299.6 1.5 fusion.107
  (11 shorter events, 0.1 us)
Async XLA Ops:
  6.5 293.0 %copy-start = (bf16[1024,1024]{1,0:T(8,128)(2,1)S(1)}, bf16[1024,1024]{1,0:T(8,128)(2,1)}, u32[]{:S(2)}) copy-start(bf16[1024,1024]{1,0:T(8,128)(2,1)} %param.8) | copy-start | bytes 6291460
  10.2 53.8 %all-to-all-start = ((bf16[8,256,1024]{2,1,0:T(8,128)(2,1)}), bf16[8,256,1024]{2,1,0:T(8,128)(2,1)}, u32[]{:S(2)}, u32[]{:S(2)}) async-start(bf16[8,256,1024]{2,1,0:T(8,128)(2,1)} %stack.3), calls=%async_computation | async-start | bytes 8388608 | tf_op jit(solution)/shard_map/all_to_all | solution.py:27
  16.2 153.0 %all-gather.2.cloned.1.call-start = ((), (), s32[]{:S(2)}) async-start(), calls=%async_computation.2 | async-start | bytes 17825792 | tf_op jit(solution)/shard_map/all_gather | solution.py:34
  68.0 1.2 copy-start.1
Sparse Core Ops, SparseCore 0:
  70.4 98.7 all-gather.1
